TPU v7x, 32 devices: a whole 2x2x4 slice. The times are simulated.
32 devices in a mesh: groups: 2 (over y), coord: 16 (over z, x, core).
Axes of the slice: x: 2, y: 2, z: 4, core: 2. Of those that a mesh axis runs over, the one named last changes fastest.
Arguments:
- activations: bfloat16 [64, 128, 4096], P(('groups', 'coord')), parts along dimension 0, may hold values from -6 to 6
- out_grads: bfloat16 [64, 128, 4096], P(('groups', 'coord')), parts along dimension 0, may hold values from -6 to 6
- proj_in: bfloat16 [4096, 128], P('coord'), may hold values from -0.09375 to 0.09375
- proj_out: bfloat16 [4096, 128], P('coord'), may hold values from -0.09375 to 0.09375
- cov_in: float32 [128, 128], replicated
- cov_out: float32 [128, 128], replicated
- lengths: int32 [64], P(('groups', 'coord')), parts along dimension 0, may hold values from 1 to 128
- seq_ids: int32 [64], P(('groups', 'coord')), parts along dimension 0, may hold values from 0 to 31, each once
- bank: bfloat16 [1536, 16384], P(None, 'coord'), may hold values from -0.015625 to 0.015625
Outputs:
- scores: bfloat16 [64, 1536], P('groups', 'coord'), parts along dimension 0
There are 2 independent parts, one for each index of `groups`. A program takes and returns all parts, laid end to end along the dimension named above; an argument that names none is the same for every part. Nothing has to cross between parts.
All inputs are finite; a program needn't handle non-finite values.
Results may differ from a plain program's by a relative error of at most 0.0064.
Values may be sent and summed in bfloat16 or wider, within the bound.
A program may use at most 128 MiB of HBM per device.

v0:
```python
import jax
import jax.numpy as jnp
from jax import lax
from jax.sharding import PartitionSpec as P


def inverse_factor(cov):
    size = cov.shape[0]
    damping = 0.1 * jnp.trace(cov) / size
    eye = jnp.eye(size, dtype=jnp.float32)
    lower = jnp.linalg.cholesky(cov + damping * eye)
    return jax.scipy.linalg.cho_solve((lower, True), eye)


def body(activations, out_grads, proj_in, proj_out, cov_in, cov_out, lengths, seq_ids, bank):
    full_in, full_out = (
        lax.all_gather(proj_in, "coord", axis=0, tiled=True),
        lax.all_gather(proj_out, "coord", axis=0, tiled=True),
    )
    seq_dev, length, width = activations.shape
    rank = full_in.shape[1]
    x_full = jnp.dot(
        activations.reshape(seq_dev * length, width), full_in, preferred_element_type=jnp.float32
    ).reshape(seq_dev, length, rank)
    position = lax.broadcasted_iota(jnp.int32, (seq_dev, length), 1)
    valid = (position < lengths[:, None]).astype(jnp.float32)
    x_proj = (x_full * valid[:, :, None]).astype(jnp.bfloat16)
    d_proj = (
        jnp.dot(
            out_grads.reshape(seq_dev * length, width), full_out, preferred_element_type=jnp.float32
        )
        .reshape(seq_dev, length, rank)
        .astype(jnp.bfloat16)
    )
    grads = jnp.einsum("sto,sti->soi", d_proj, x_proj, preferred_element_type=jnp.float32)
    k_in = inverse_factor(cov_in)
    k_out = inverse_factor(cov_out)
    left = jnp.einsum("ab,sbc->sac", k_out, grads, precision=lax.Precision.HIGHEST)
    whitened = jnp.einsum("sac,cd->sad", left, k_in, precision=lax.Precision.HIGHEST)
    whitened = whitened.astype(jnp.bfloat16).reshape(seq_dev, rank * rank)
    all_ids = lax.all_gather(seq_ids, "coord", axis=0, tiled=True)
    columns = lax.all_to_all(whitened, "coord", split_axis=1, concat_axis=0, tiled=True)
    summed = lax.psum_scatter(
        lax.dot_general(
            bank, columns, (((1,), (1,)), ((), ())), preferred_element_type=jnp.float32
        ),
        "coord",
        scatter_dimension=0,
        tiled=True,
    )
    raw = summed.T.astype(jnp.bfloat16)
    return jnp.zeros_like(raw).at[all_ids].set(raw)


def solution(mesh):
    in_specs = (
        P(("groups", "coord"), None, None),
        P(("groups", "coord"), None, None),
        P("coord", None),
        P("coord", None),
        P(),
        P(),
        P(("groups", "coord")),
        P(("groups", "coord")),
        P(None, "coord"),
    )
    out_specs = P("groups", "coord")
    return jax.shard_map(body, mesh=mesh, in_specs=in_specs, out_specs=out_specs, check_vma=False)
```

profile of v0, /device:TPU:0, one launch (start us, length us, event | category | flops | bytes accessed | tf_op | source)
XLA Modules:
  0.0 168.9 jit_solution(12148271944048150464)
XLA Ops:
  6.5 0.7 all-gather.3.cloned.1.call-update
  7.3 0.7 all-gather.5.cloned.1.call-update
  8.1 0.9 copy.25
  9.0 0.6 select_reduce_fusion.3
  10.4 11.7 %cholesky.44 = f32[128,128]{1,0:T(8,128)S(1)} custom-call(f32[128,128]{1,0:T(8,128)S(1)} %fusion.16), custom_call_target="Cholesky" | custom-call | tf_op jit(solution)/shard_map/jit(cholesky)/cholesky | solution.py:11
  22.2 0.6 compare_reduce_fusion.1
  22.8 0.7 fusion.9
  23.5 0.9 copy.29
  24.4 0.6 select_reduce_fusion.2
  25.7 9.8 %custom-call.8 = f32[1,128,128]{1,2,0:T(8,128)S(1)} custom-call(f32[1,128,128]{2,1,0:T(8,128)S(1)} %fusion.9), custom_call_target="InvertDiagBlocksLowerTriangular" | custom-call | tf_op jit(solution)/shard_map/jit(_cho_solve)/triangular_solve | solution.py:12
  35.6 11.7 %cholesky.55 = f32[128,128]{1,0:T(8,128)S(1)} custom-call(f32[128,128]{1,0:T(8,128)S(1)} %fusion.13), custom_call_target="Cholesky" | custom-call | tf_op jit(solution)/shard_map/jit(cholesky)/cholesky | solution.py:11
  47.4 0.6 compare_reduce_fusion
  48.0 0.7 fusion.10
  48.7 9.9 %custom-call.9 = f32[1,128,128]{1,2,0:T(8,128)S(1)} custom-call(f32[1,128,128]{2,1,0:T(8,128)S(1)} %fusion.10), custom_call_target="InvertDiagBlocksLowerTriangular" | custom-call | tf_op jit(solution)/shard_map/jit(_cho_solve)/triangular_solve | solution.py:12
  59.7 2.6 %convolution_convert_fusion = bf16[2,128,128]{2,1,0:T(8,128)(2,1)S(1)} fusion(bf16[2,128,4096]{2,1,0:T(8,128)(2,1)} %param.13, bf16[4096,128]{1,0:T(8,128)(2,1)} %all-gather.3.cloned.1.call-done), kind=kOutput, calls=%fused_computation.4 | convolution fusion | flops 268468224 | bytes 3211264 | tf_op jit(solution)/shard_map/dot_general | solution.py:29
  62.3 27.5 %all-gather.5.cloned.1.call-done = bf16[4096,128]{1,0:T(8,128)(2,1)} async-done(((bf16[256,128]{1,0:T(8,128)(2,1)}), bf16[4096,128]{1,0:T(8,128)(2,1)}) %all-gather.5.cloned.1.call-update) | async-done | bytes 1048592 | tf_op jit(solution)/shard_map/all_gather | solution.py:17
  89.8 2.7 %fusion.1 = f32[2,128,128]{1,2,0:T(8,128)S(1)} fusion(bf16[2,128,128]{2,1,0:T(8,128)(2,1)S(1)} %convolution_convert_fusion, bf16[2,128,4096]{2,1,0:T(8,128)(2,1)} %param.12, bf16[4096,128]{1,0:T(8,128)(2,1)} %all-gather.5.cloned.1.call-done, f32[2,128]{1,0:T(2,128)S(1)} %compare_convert_fusion), kind=kOutput, calls=%fused_computation.7 | convolution fusion | flops 276889600 | bytes 3343360 | tf_op jit(solution)/shard_map/sto,sti->soi/dot_general | solution.py:35
  93.4 10.4 %all_to_all.19 = bf16[2,16,1024]{2,0,1:T(2,128)(2,1)S(1)} all-to-all(bf16[2,16,1024]{2,0,1:T(2,128)(2,1)S(1)} %copy.32), channel_id=1, replica_groups=mesh['groups'=2,'coord'=16] {'coord'}, dimensions={1} | all-to-all | bytes 131072 | tf_op jit(solution)/shard_map/all_to_all | solution.py:42
  103.8 1.0 convolution_bitcast_fusion
  104.8 1.2 copy.36
  107.5 8.6 %all-reduce = s32[32]{0:T(128)S(1)} all-reduce(s32[32]{0:T(128)S(1)} %dynamic-update-slice.2), channel_id=1, replica_groups=mesh['groups'=2,'coord'=16] {'coord'}, use_global_device_ids=true, to_apply=%add | all-reduce | flops 32 | bytes 256
  116.1 44.2 %reduce-scatter.4.cloned.1.call-done = f32[96,32]{1,0:T(8,128)} async-done(((f32[1536,32]{1,0:T(8,128)}), f32[96,32]{1,0:T(8,128)}) %reduce-scatter.4.cloned.1.call-update) | async-done | bytes 12304
  160.3 0.9 copy.37
  161.1 1.2 scatter_custom_fusion
  (35 shorter events, 3.1 us)
Async XLA Ops:
  6.5 97.2 %copy-start = (bf16[1536,1024]{1,0:T(8,128)(2,1)S(1)}, bf16[1536,1024]{1,0:T(8,128)(2,1)}, u32[]{:S(2)}) copy-start(bf16[1536,1024]{1,0:T(8,128)(2,1)} %param.20) | copy-start | bytes 9437188
  6.5 53.1 %copy-start.1 = (s32[2]{0:T(128)S(1)}, s32[2]{0:T(128)}, u32[]{:S(2)}) copy-start(s32[2]{0:T(128)} %param.18) | copy-start | bytes 28
  6.5 53.2 %all-gather.3.cloned.1.call-start = ((), (), s32[]{:S(2)}) async-start(), calls=%async_computation.2 | async-start | bytes 1114112 | tf_op jit(solution)/shard_map/all_gather | solution.py:18
  7.3 82.6 %all-gather.5.cloned.1.call-start = ((), (), s32[]{:S(2)}) async-start(), calls=%async_computation.3 | async-start | bytes 1114112 | tf_op jit(solution)/shard_map/all_gather | solution.py:17
  8.0 152.3 %reduce-scatter.4.cloned.1.call-start = ((), (), s32[]{:S(2)}) async-start(), calls=%async_computation.4 | async-start | bytes 835584
  103.8 2.2 %copy-start.3 = (u32[32]{0:T(128)S(1)}, u32[32]{0:T(128)}, u32[]{:S(2)}) copy-start(u32[32]{0:T(128)} %constant.63) | copy-start | bytes 388
  103.8 3.5 %copy-start.2 = (s32[2]{0:T(128)S(1)}, s32[2]{0:T(128)}, u32[]{:S(2)}) copy-start(s32[2]{0:T(128)} %param.19) | copy-start | bytes 28
Sparse Core Ops, SparseCore 0:
  9.5 41.1 all-gather.2
  52.9 36.9 all-gather.4
  106.1 54.0 reduce-scatter.3
where the time goes:
time: 169 us
  waiting for transfers between devices  73.1 us (43%)
  other arithmetic  48.5 us (29%)
  blocking collectives  18.9 us (11%)
  between operations  15.3 us (9%)
  matrix products  7.97 us (5%)
  local copies, waits for them, and re-layouts  5.04 us (3%)
    unnamed x4, waiting for transfers between devices  45.6 us
    all_gather x1, waiting for transfers between devices, body(): lax.all_gather(proj_in, 'coord', axis=0, tiled=True)  27.5 us
    another operation x6, other arithmetic, inverse_factor(): lower = jnp.linalg.cholesky(cov + damping * eye)  24.8 us
    another operation x4, other arithmetic, inverse_factor(): return jax.scipy.linalg.cho_solve((lower, True), eye)  21.1 us
    all_to_all x1, blocking collectives, body(): lax.all_to_all(whitened, 'coord', split_axis=1, concat_axis=0, tiled=True)  10.4 us
    unnamed x1, blocking collectives  8.57 us
    unnamed x15, local copies, waits for them, and re-layouts  4.73 us
  transfers between devices with their start and end apart: 3, of which 2 were waited for; matrix products, arithmetic and copies ran while one was open for 32% of the time, Pallas kernels for 0%

commit v1 on v0

v1 whole, which is shorter than its diff:
```python
import functools

import jax
import jax.numpy as jnp
from jax import lax
from jax.experimental import pallas as pl
from jax.experimental.pallas import tpu as pltpu
from jax.sharding import PartitionSpec as P

MESH = pl.DeviceIdType.MESH
F32 = jnp.float32
BF16 = jnp.bfloat16
PANEL = 8


def xor(value, mask):
    bit = 1
    result = value
    while bit <= mask:
        if mask & bit:
            result = result + bit - 2 * bit * ((value // bit) % 2)
        bit *= 2
    return result


def start_factor(cov):
    size = cov.shape[0]
    rows = lax.broadcasted_iota(jnp.int32, (size, size), 0)
    lanes = lax.broadcasted_iota(jnp.int32, (size, size), 1)
    diagonal = jnp.where(rows == lanes, cov, 0.0)
    damping = 0.1 * jnp.sum(diagonal) / size
    return jnp.where(rows == lanes, cov + damping, cov)


def eliminate_panel(matrix):
    size = matrix.shape[0]
    top, rest = matrix[:PANEL], matrix[PANEL:]
    lane = lax.broadcasted_iota(jnp.int32, (1, size), 1)
    sub = lax.broadcasted_iota(jnp.int32, (PANEL, 1), 0)
    for r in range(PANEL):
        row = top[r : r + 1]
        inverse = 1.0 / row[:, r : r + 1]
        scaled = jnp.where(lane == r, inverse, row * inverse)
        top_new = jnp.where(lane == r, 0.0, top) - top[:, r : r + 1] * scaled
        rest = jnp.where(lane == r, 0.0, rest) - rest[:, r : r + 1] * scaled
        top = jnp.where(sub == r, scaled, top_new)
    whole = jnp.concatenate([rest, top], axis=0)
    return pltpu.roll(whole, size - PANEL, 1)


def kernel(
    n, slow, fast,
    act_ref, og_ref, pin_ref, pout_ref, cin_ref, cout_ref, len_ref, ids_ref, bank_ref,
    out_ref,
    act, og, bank, g, k, idbuf, wsend, wrecv, psend, precv,
    load_sem, gs_sem, gr_sem, is_sem, ir_sem, ws_sem, wr_sem, ps_sem, pr_sem,
):
    group = lax.axis_index("groups")
    me = lax.axis_index("coord")
    seqs = len_ref.shape[0]
    length = act.shape[0] // seqs
    rank = cin_ref.shape[0]
    shard = pin_ref.shape[0]
    queries = out_ref.shape[1]
    per = bank_ref.shape[1] // rank
    block = wsend.shape[1]

    loads = [
        pltpu.make_async_copy(pin_ref, g.at[me, 0], load_sem.at[0]),
        pltpu.make_async_copy(pout_ref, g.at[me, 1], load_sem.at[1]),
        pltpu.make_async_copy(act_ref, act, load_sem.at[2]),
        pltpu.make_async_copy(og_ref, og, load_sem.at[3]),
        pltpu.make_async_copy(bank_ref, bank.at[pl.ds(0, bank_ref.shape[0])], load_sem.at[4]),
    ]
    for load in loads:
        load.start()

    barrier = pltpu.get_barrier_semaphore()
    for j in range(1, n):
        pl.semaphore_signal(barrier, inc=1, device_id=(group, xor(me, j)), device_id_type=MESH)

    for s in range(seqs):
        idbuf[me, s : s + 1] = jnp.full((1, idbuf.shape[2]), ids_ref[s], jnp.int32)
    k[0] = start_factor(cin_ref[...])
    k[1] = start_factor(cout_ref[...])
    tail = bank.shape[0] - bank_ref.shape[0]
    if tail:
        bank[bank_ref.shape[0] :] = jnp.zeros((tail, bank.shape[1]), BF16)
    if block > seqs * per:
        wsend[...] = jnp.zeros_like(wsend)

    loads[0].wait()
    loads[1].wait()
    pl.semaphore_wait(barrier, n - 1)

    gathers = []

    def send(slot_mask, to_mask):
        slot = xor(me, slot_mask)
        copy = pltpu.make_async_remote_copy(
            src_ref=g.at[slot], dst_ref=g.at[slot],
            send_sem=gs_sem.at[len(gathers)], recv_sem=gr_sem.at[slot],
            device_id=(group, xor(me, to_mask)), device_id_type=MESH,
        )
        copy.start()
        gathers.append(copy)

    def arrived(slot_mask):
        slot = xor(me, slot_mask)
        pltpu.make_async_remote_copy(
            src_ref=g.at[slot], dst_ref=g.at[slot],
            send_sem=gs_sem.at[0], recv_sem=gr_sem.at[slot],
            device_id=(group, xor(me, 1)), device_id_type=MESH,
        ).wait_recv()

    fasts = [2 * b for b in range(1, fast)]
    slows = [2 * fast * a for a in range(1, slow)]
    for mask in fasts + slows:
        send(0, mask)
    send(0, 1)

    id_copies = []
    for j in range(1, n):
        copy = pltpu.make_async_remote_copy(
            src_ref=idbuf.at[me], dst_ref=idbuf.at[me],
            send_sem=is_sem.at[j], recv_sem=ir_sem.at[j],
            device_id=(group, xor(me, j)), device_id_type=MESH,
        )
        copy.start()
        id_copies.append(copy)

    def from_slow(mask):
        arrived(mask)
        for b in fasts:
            send(mask, b)
        send(mask, 1)

    def from_fast(mask):
        for b in fasts:
            arrived(mask + b)
            send(mask + b, 1)

    events = []
    for a in range(slow):
        if a + 1 < slow:
            events.append((from_slow, slows[a]))
        events.append((from_fast, slows[a - 1] if a else 0))

    panels = rank // PANEL

    def step(_, carry):
        first, second = k[0], k[1]
        k[0] = eliminate_panel(first)
        k[1] = eliminate_panel(second)
        return carry

    done = 0
    for at, (event, mask) in enumerate(events):
        upto = panels * (at + 1) // len(events)
        if upto > done:
            lax.fori_loop(0, upto - done, step, 0)
            done = upto
        event(mask)

    loads[2].wait()
    loads[3].wait()
    for mask in [0] + slows:
        for b in [0] + fasts:
            arrived(mask + b + 1)

    join = max(1, 256 // shard)
    x_full = jnp.zeros((seqs * length, rank), F32)
    d_full = jnp.zeros((seqs * length, rank), F32)
    for o in range(0, n, join):
        columns = slice(o * shard, (o + join) * shard)
        x_full += jnp.dot(
            act[:, columns], g[o : o + join, 0].reshape(join * shard, rank), preferred_element_type=F32
        )
        d_full += jnp.dot(
            og[:, columns], g[o : o + join, 1].reshape(join * shard, rank), preferred_element_type=F32
        )
    position = lax.broadcasted_iota(jnp.int32, (length, 1), 0)
    for s in range(seqs):
        rows = slice(s * length, (s + 1) * length)
        valid = (position < len_ref[s]).astype(F32)
        x_proj = (x_full[rows] * valid).astype(BF16)
        d_proj = d_full[rows].astype(BF16)
        grads = lax.dot_general(d_proj, x_proj, (((0,), (0,)), ((), ())), preferred_element_type=F32)
        left = jnp.dot(k[1], grads, precision=lax.Precision.HIGHEST, preferred_element_type=F32)
        white = jnp.dot(left, k[0], precision=lax.Precision.HIGHEST, preferred_element_type=F32)
        wsend[:, s * per : (s + 1) * per] = white.reshape(n, per, rank)

    def exchange(src, dst, send_sem, recv_sem, j):
        copy = pltpu.make_async_remote_copy(
            src_ref=src, dst_ref=dst,
            send_sem=send_sem.at[j], recv_sem=recv_sem.at[j],
            device_id=(group, xor(me, j)), device_id_type=MESH,
        )
        copy.start()
        return copy

    mine = pl.ds(pl.multiple_of(me * block, block), block)
    white_copies = [
        exchange(wsend.at[xor(me, j)], wrecv.at[mine], ws_sem, wr_sem, j) for j in range(n - 1, 0, -1)
    ]
    wrecv[mine] = wsend[me]
    loads[4].wait()
    for copy in white_copies:
        copy.wait_recv()
    for copy in id_copies:
        copy.wait_recv()

    columns = jnp.concatenate(
        [
            jnp.concatenate(
                [wrecv[pl.ds(s * per + a, n, stride=block), :] for s in range(seqs)], axis=0
            ).astype(BF16)
            for a in range(per)
        ],
        axis=1,
    )

    def partial(target):
        rows = bank[pl.ds(pl.multiple_of(target * queries, queries), psend.shape[2])]
        return lax.dot_general(columns, rows, (((1,), (1,)), ((), ())), preferred_element_type=F32)

    score_copies = []
    for j in range(n - 1, 0, -1):
        psend[j] = partial(xor(me, j)).astype(BF16)
        score_copies.append(exchange(psend.at[j], precv.at[j], ps_sem, pr_sem, j))
    total = partial(me)
    ids = jnp.concatenate([idbuf[:, s, :] for s in range(seqs)], axis=0)[:, :1]
    held = n * seqs
    one_hot = (ids == lax.broadcasted_iota(jnp.int32, (held, held), 1)).astype(BF16)
    for copy in score_copies:
        copy.wait_recv()
    for j in range(n - 1, 0, -1):
        total += precv[j].astype(F32)
    placed = lax.dot_general(
        one_hot, total.astype(BF16), (((0,), (0,)), ((), ())), preferred_element_type=F32
    )
    out_ref[...] = placed[:, :queries].astype(BF16)
    for copy in gathers + id_copies + white_copies + score_copies:
        copy.wait_send()


def solution(mesh):
    n = mesh.shape["coord"]
    chips = n // 2
    slow = 1
    while slow * slow < chips:
        slow *= 2
    fast = chips // slow

    def body(activations, out_grads, proj_in, proj_out, cov_in, cov_out, lengths, seq_ids, bank):
        seqs, length, width = activations.shape
        shard, rank = proj_in.shape
        per = bank.shape[1] // rank
        queries = bank.shape[0] // n
        wide = -(-queries // 128) * 128
        block = -(-(seqs * per) // 8) * 8
        held = n * seqs
        vmem = pl.BlockSpec(memory_space=pltpu.VMEM)
        smem = pl.BlockSpec(memory_space=pltpu.SMEM)
        hbm = pl.BlockSpec(memory_space=pl.ANY)
        dma = pltpu.SemaphoreType.DMA
        return pl.pallas_call(
            functools.partial(kernel, n, slow, fast),
            out_shape=jax.ShapeDtypeStruct((held, queries), BF16),
            in_specs=[hbm, hbm, hbm, hbm, vmem, vmem, smem, smem, hbm],
            out_specs=vmem,
            scratch_shapes=[
                pltpu.VMEM((seqs * length, width), BF16),
                pltpu.VMEM((seqs * length, width), BF16),
                pltpu.VMEM((bank.shape[0] + wide - queries, bank.shape[1]), BF16),
                pltpu.VMEM((n, 2, shard, rank), BF16),
                pltpu.VMEM((2, rank, rank), F32),
                pltpu.VMEM((n, seqs, 128), jnp.int32),
                pltpu.VMEM((n, block, rank), F32),
                pltpu.VMEM((n * block, rank), F32),
                pltpu.VMEM((n, held, wide), BF16),
                pltpu.VMEM((n, held, wide), BF16),
                dma((5,)),
                dma((n,)), dma((n,)), dma((n,)), dma((n,)),
                dma((n,)), dma((n,)), dma((n,)), dma((n,)),
            ],
            compiler_params=pltpu.CompilerParams(collective_id=0, has_side_effects=True),
        )(
            activations.reshape(seqs * length, width), out_grads.reshape(seqs * length, width),
            proj_in, proj_out, cov_in, cov_out, lengths, seq_ids, bank,
        )

    in_specs = (
        P(("groups", "coord"), None, None),
        P(("groups", "coord"), None, None),
        P("coord", None),
        P("coord", None),
        P(),
        P(),
        P(("groups", "coord")),
        P(("groups", "coord")),
        P(None, "coord"),
    )
    return jax.shard_map(body, mesh=mesh, in_specs=in_specs, out_specs=P("groups", "coord"), check_vma=False)
```

time: 169 us -> 43.5 us (0.26)
  waiting for transfers between devices: 73.1 us -> 0 us
  other arithmetic: 48.5 us -> 0 us
  Pallas kernels: 0 us -> 41.9 us
  blocking collectives: 18.9 us -> 0 us
  between operations: 15.3 us -> 0.01 us
  matrix products: 7.97 us -> 0 us
  local copies, waits for them, and re-layouts: 5.04 us -> 1.3 us
    another operation x10 -> x0, other arithmetic: 45.9 us -> none  [the longest x6 24.8 us: inverse_factor(): lower = jnp.linalg.cholesky(cov + damping * eye)]
    unnamed x4 -> x0, waiting for transfers between devices: 45.6 us -> none
    pallas_call x0 -> x1, Pallas kernels: none -> 41.9 us  [body(): pl.pallas_call(functools.partial(kernel, n, slow, fast), out_shape=jax.Sh...]
    all_gather x2 -> x0, waiting for transfers between devices: 27.5 us -> none  [the longest x1 27.5 us: body(): lax.all_gather(proj_in, 'coord', axis=0, tiled=True)]
    all_to_all x1 -> x0, blocking collectives: 10.4 us -> none  [body(): lax.all_to_all(whitened, 'coord', split_axis=1, concat_axis=0, tiled=True)]
    unnamed x1 -> x0, blocking collectives: 8.57 us -> none
    dot_general x5 -> x0, matrix products: 6.99 us -> none  [the longest x1 2.73 us: body(): jnp.einsum('sto,sti->soi', d_proj, x_proj, preferred_element_type=jnp.flo...]
    unnamed x15 -> x1, local copies, waits for them, and re-layouts: 4.73 us -> 1.3 us
  transfers between devices with their start and end apart: 3 -> 0, of which waited for: 2 -> 0; matrix products, arithmetic and copies ran while one was open for 32% -> 0% of each run, Pallas kernels for 0% -> 0%
where the time goes in v1:
time: 43.5 us; the launch traced here: 43.2 us
  Pallas kernels  41.9 us (96%)
  local copies, waits for them, and re-layouts  1.3 us (3%)
    pallas_call x1, Pallas kernels, body(): pl.pallas_call(functools.partial(kernel, n, slow, fast), out_shape=jax.Sh...  41.9 us
    unnamed x1, local copies, waits for them, and re-layouts  1.3 us

profile of v1, /device:TPU:0, one launch (start us, length us, event | category | flops | bytes accessed | tf_op | source)
XLA Modules:
  0.0 43.2 jit_solution(8447624091541366127)
XLA Ops:
  0.0 41.9 %shard_map.91 = bf16[32,96]{1,0:T(8,128)(2,1)} custom-call(bf16[256,4096]{1,0:T(8,128)(2,1)} %bitcast.2, bf16[256,4096]{1,0:T(8,128)(2,1)} %bitcast.3, bf16[256,128]{1,0:T(8,128)(2,1)} %pin_ref.1, bf16[256,128]{1,0:T(8,128)(2,1)} %pout_ref.1, f32[128,128]{1,0:T(8,128)} %cin_ref.1, f32[128,128]{1,0:T(8,128)} %cout_ref.1, s32[2]{0:T(128)} %len_ref.1, ...), custom_call_target="tpu_custom_call" | custom-call | tf_op jit(solution)/shard_map/pallas_call | solution.py:267
  42.0 1.3 %copy.11 = bf16[32,96]{1,0:T(8,128)(2,1)} copy(bf16[32,96]{1,0:T(8,128)(2,1)} %shard_map.91) | data formatting | bytes 12288

commit v2 on v1

--- a/solution.py
+++ b/solution.py
@@ -35,24 +35,34 @@
 def eliminate_panel(matrix):
     size = matrix.shape[0]
     top, rest = matrix[:PANEL], matrix[PANEL:]
-    lane = lax.broadcasted_iota(jnp.int32, (1, size), 1)
-    sub = lax.broadcasted_iota(jnp.int32, (PANEL, 1), 0)
+    lane = lax.broadcasted_iota(jnp.int32, (PANEL, size), 1)
+    sub = lax.broadcasted_iota(jnp.int32, (PANEL, size), 0)
+    pivots = [jnp.broadcast_to(top[:, r : r + 1], (PANEL, size)) for r in range(PANEL)]
+    top = jnp.where(lane < PANEL, jnp.where(lane == sub, 1.0, 0.0), top)
     for r in range(PANEL):
-        row = top[r : r + 1]
-        inverse = 1.0 / row[:, r : r + 1]
-        scaled = jnp.where(lane == r, inverse, row * inverse)
-        top_new = jnp.where(lane == r, 0.0, top) - top[:, r : r + 1] * scaled
-        rest = jnp.where(lane == r, 0.0, rest) - rest[:, r : r + 1] * scaled
-        top = jnp.where(sub == r, scaled, top_new)
+        factor = pivots[r]
+        inverse = 1.0 / factor[r : r + 1]
+
+        def reduced(value):
+            scaled = value[r : r + 1] * inverse
+            return jnp.where(sub == r, scaled, value - factor * scaled)
+
+        top = reduced(top)
+        for later in range(r + 1, PANEL):
+            pivots[later] = reduced(pivots[later])
+    column = rest
+    rest = jnp.where(lane[:1] < PANEL, 0.0, rest)
+    for r in range(PANEL):
+        rest = rest - column[:, r : r + 1] * top[r : r + 1]
     whole = jnp.concatenate([rest, top], axis=0)
     return pltpu.roll(whole, size - PANEL, 1)
 
 
 def kernel(
     n, slow, fast,
-    act_ref, og_ref, pin_ref, pout_ref, cin_ref, cout_ref, len_ref, ids_ref, bank_ref,
-    out_ref,
-    act, og, bank, g, k, idbuf, wsend, wrecv, psend, precv,
+    act_ref, og_ref, pin_ref, pout_ref, cin_ref, cout_ref, len_hbm, ids_hbm, bank_ref,
+    out_ref, len_ref, ids_ref,
+    act, og, bank, g, k, x_full, d_full, idbuf, wsend, wrecv, psend, precv,
     load_sem, gs_sem, gr_sem, is_sem, ir_sem, ws_sem, wr_sem, ps_sem, pr_sem,
 ):
     group = lax.axis_index("groups")
@@ -71,53 +81,71 @@
         pltpu.make_async_copy(act_ref, act, load_sem.at[2]),
         pltpu.make_async_copy(og_ref, og, load_sem.at[3]),
         pltpu.make_async_copy(bank_ref, bank.at[pl.ds(0, bank_ref.shape[0])], load_sem.at[4]),
+        pltpu.make_async_copy(cin_ref, k.at[0], load_sem.at[5]),
+        pltpu.make_async_copy(cout_ref, k.at[1], load_sem.at[6]),
+        pltpu.make_async_copy(len_hbm, len_ref, load_sem.at[7]),
+        pltpu.make_async_copy(ids_hbm, ids_ref, load_sem.at[8]),
     ]
-    for load in loads:
+    for load in loads[:2] + loads[5:] + loads[2:5]:
         load.start()
 
     barrier = pltpu.get_barrier_semaphore()
+    pl.semaphore_signal(barrier, inc=1, device_id=(1 - group, me), device_id_type=MESH)
     for j in range(1, n):
         pl.semaphore_signal(barrier, inc=1, device_id=(group, xor(me, j)), device_id_type=MESH)
 
+    loads[0].wait()
+    loads[1].wait()
+    pl.semaphore_wait(barrier, n)
+
+    gathers = []
+    own, other = group, 1 - group
+
+    def send(slot_mask, piece, to):
+        slot = xor(me, slot_mask)
+        copy = pltpu.make_async_remote_copy(
+            src_ref=g.at[slot, piece], dst_ref=g.at[slot, piece],
+            send_sem=gs_sem.at[len(gathers)], recv_sem=gr_sem.at[slot, piece],
+            device_id=to, device_id_type=MESH,
+        )
+        copy.start()
+        gathers.append(copy)
+
+    def arrived(slot_mask, piece):
+        slot = xor(me, slot_mask)
+        pltpu.make_async_remote_copy(
+            src_ref=g.at[slot, piece], dst_ref=g.at[slot, piece],
+            send_sem=gs_sem.at[0], recv_sem=gr_sem.at[slot, piece],
+            device_id=(group, xor(me, 1)), device_id_type=MESH,
+        ).wait_recv()
+
+    def peer(mask):
+        return (group, xor(me, mask))
+
+    sibling, twin = peer(1), (other, me)
+    fasts = [2 * b for b in range(1, fast)]
+    slows = [2 * fast * a for a in range(1, slow)]
+    early = slows[:1]
+    for mask in fasts:
+        send(0, own, peer(mask))
+    for mask in slows:
+        send(0, own, peer(mask))
+    for mask in fasts:
+        send(0, other, peer(mask))
+    send(0, own, sibling)
+    send(0, other, sibling)
+
+    for load in loads[5:]:
+        load.wait()
     for s in range(seqs):
         idbuf[me, s : s + 1] = jnp.full((1, idbuf.shape[2]), ids_ref[s], jnp.int32)
-    k[0] = start_factor(cin_ref[...])
-    k[1] = start_factor(cout_ref[...])
+    k[0] = start_factor(k[0])
+    k[1] = start_factor(k[1])
     tail = bank.shape[0] - bank_ref.shape[0]
     if tail:
         bank[bank_ref.shape[0] :] = jnp.zeros((tail, bank.shape[1]), BF16)
     if block > seqs * per:
         wsend[...] = jnp.zeros_like(wsend)
-
-    loads[0].wait()
-    loads[1].wait()
-    pl.semaphore_wait(barrier, n - 1)
-
-    gathers = []
-
-    def send(slot_mask, to_mask):
-        slot = xor(me, slot_mask)
-        copy = pltpu.make_async_remote_copy(
-            src_ref=g.at[slot], dst_ref=g.at[slot],
-            send_sem=gs_sem.at[len(gathers)], recv_sem=gr_sem.at[slot],
-            device_id=(group, xor(me, to_mask)), device_id_type=MESH,
-        )
-        copy.start()
-        gathers.append(copy)
-
-    def arrived(slot_mask):
-        slot = xor(me, slot_mask)
-        pltpu.make_async_remote_copy(
-            src_ref=g.at[slot], dst_ref=g.at[slot],
-            send_sem=gs_sem.at[0], recv_sem=gr_sem.at[slot],
-            device_id=(group, xor(me, 1)), device_id_type=MESH,
-        ).wait_recv()
-
-    fasts = [2 * b for b in range(1, fast)]
-    slows = [2 * fast * a for a in range(1, slow)]
-    for mask in fasts + slows:
-        send(0, mask)
-    send(0, 1)
 
     id_copies = []
     for j in range(1, n):
@@ -130,21 +158,78 @@
         id_copies.append(copy)
 
     def from_slow(mask):
-        arrived(mask)
+        arrived(mask, own)
         for b in fasts:
-            send(mask, b)
-        send(mask, 1)
+            send(mask, own, peer(b))
+        send(mask, own, twin)
+        send(mask, own, sibling)
 
     def from_fast(mask):
         for b in fasts:
-            arrived(mask + b)
-            send(mask + b, 1)
+            arrived(mask + b, own)
+            if mask and mask not in early:
+                send(mask + b, own, twin)
+            send(mask + b, own, sibling)
+
+    def from_twin(mask):
+        arrived(mask, other)
+        if mask in early:
+            for b in fasts:
+                send(mask, other, peer(b))
+        send(mask, other, sibling)
+
+    def last(mask):
+        for b in fasts:
+            arrived(mask + b, other)
+            send(mask + b, other, sibling)
+
+    span = n // slow * shard
+
+    def project(mask):
+        if mask == 0:
+            loads[2].wait()
+            loads[3].wait()
+        for b in [0] + fasts:
+            for piece in (own, other):
+                arrived(mask + b + 1, piece)
+        block_at = xor(me // (2 * fast), mask // (2 * fast))
+        columns = pl.ds(pl.multiple_of(block_at * span, 128), span)
+        shards = pl.ds(block_at * 2 * fast, 2 * fast)
+        x_part = jnp.dot(
+            act[:, columns], g[shards, 0].reshape(span, rank), preferred_element_type=F32
+        )
+        d_part = jnp.dot(
+            og[:, columns], g[shards, 1].reshape(span, rank), preferred_element_type=F32
+        )
+        if mask == 0:
+            x_full[...] = x_part
+            d_full[...] = d_part
+        else:
+            x_full[...] += x_part
+            d_full[...] += d_part
 
     events = []
     for a in range(slow):
         if a + 1 < slow:
             events.append((from_slow, slows[a]))
-        events.append((from_fast, slows[a - 1] if a else 0))
+        if a + 2 == slow:
+            events.append((project, 0))
+        if a:
+            events.append((from_twin, slows[a - 1]))
+            events.append((from_fast, slows[a - 1]))
+            if a > 1:
+                events.append((last, slows[a - 2]))
+            if a > 2:
+                events.append((project, slows[a - 3]))
+        else:
+            events.append((from_fast, 0))
+            if slow > 1:
+                events.append((last, 0))
+    events.append((last, slows[-1] if slows else 0))
+    if slow == 1:
+        events.append((project, 0))
+    for mask in slows[max(0, slow - 3):]:
+        events.append((project, mask))
 
     panels = rank // PANEL
 
@@ -162,23 +247,6 @@
             done = upto
         event(mask)
 
-    loads[2].wait()
-    loads[3].wait()
-    for mask in [0] + slows:
-        for b in [0] + fasts:
-            arrived(mask + b + 1)
-
-    join = max(1, 256 // shard)
-    x_full = jnp.zeros((seqs * length, rank), F32)
-    d_full = jnp.zeros((seqs * length, rank), F32)
-    for o in range(0, n, join):
-        columns = slice(o * shard, (o + join) * shard)
-        x_full += jnp.dot(
-            act[:, columns], g[o : o + join, 0].reshape(join * shard, rank), preferred_element_type=F32
-        )
-        d_full += jnp.dot(
-            og[:, columns], g[o : o + join, 1].reshape(join * shard, rank), preferred_element_type=F32
-        )
     position = lax.broadcasted_iota(jnp.int32, (length, 1), 0)
     for s in range(seqs):
         rows = slice(s * length, (s + 1) * length)
@@ -246,6 +314,7 @@
 
 def solution(mesh):
     n = mesh.shape["coord"]
+    assert mesh.shape["groups"] == 2
     chips = n // 2
     slow = 1
     while slow * slow < chips:
@@ -261,27 +330,30 @@
         block = -(-(seqs * per) // 8) * 8
         held = n * seqs
         vmem = pl.BlockSpec(memory_space=pltpu.VMEM)
-        smem = pl.BlockSpec(memory_space=pltpu.SMEM)
         hbm = pl.BlockSpec(memory_space=pl.ANY)
         dma = pltpu.SemaphoreType.DMA
         return pl.pallas_call(
             functools.partial(kernel, n, slow, fast),
             out_shape=jax.ShapeDtypeStruct((held, queries), BF16),
-            in_specs=[hbm, hbm, hbm, hbm, vmem, vmem, smem, smem, hbm],
+            in_specs=[hbm] * 9,
             out_specs=vmem,
             scratch_shapes=[
+                pltpu.SMEM((seqs,), jnp.int32),
+                pltpu.SMEM((seqs,), jnp.int32),
                 pltpu.VMEM((seqs * length, width), BF16),
                 pltpu.VMEM((seqs * length, width), BF16),
                 pltpu.VMEM((bank.shape[0] + wide - queries, bank.shape[1]), BF16),
                 pltpu.VMEM((n, 2, shard, rank), BF16),
                 pltpu.VMEM((2, rank, rank), F32),
+                pltpu.VMEM((seqs * length, rank), F32),
+                pltpu.VMEM((seqs * length, rank), F32),
                 pltpu.VMEM((n, seqs, 128), jnp.int32),
                 pltpu.VMEM((n, block, rank), F32),
                 pltpu.VMEM((n * block, rank), F32),
                 pltpu.VMEM((n, held, wide), BF16),
                 pltpu.VMEM((n, held, wide), BF16),
-                dma((5,)),
-                dma((n,)), dma((n,)), dma((n,)), dma((n,)),
+                dma((9,)),
+                dma((2 * n,)), dma((n, 2)), dma((n,)), dma((n,)),
                 dma((n,)), dma((n,)), dma((n,)), dma((n,)),
             ],
             compiler_params=pltpu.CompilerParams(collective_id=0, has_side_effects=True),

time: 43.5 us -> 40.1 us (0.922)
  Pallas kernels: 41.9 us -> 38.6 us
    pallas_call x1, Pallas kernels: 41.9 us -> 38.6 us  [body(): pl.pallas_call(functools.partial(kernel, n, slow, fast), out_shape=jax.Sh...]
where the time goes in v2:
time: 40.1 us; the launch traced here: 39.9 us
  Pallas kernels  38.6 us (96%)
  local copies, waits for them, and re-layouts  1.3 us (3%)
    pallas_call x1, Pallas kernels, body(): pl.pallas_call(functools.partial(kernel, n, slow, fast), out_shape=jax.Sh...  38.6 us
    unnamed x1, local copies, waits for them, and re-layouts  1.3 us

profile of v2, /device:TPU:0, one launch (start us, length us, event | category | flops | bytes accessed | tf_op | source)
XLA Modules:
  0.0 39.9 jit_solution(16053603253012271702)
XLA Ops:
  0.0 38.6 %shard_map.91 = bf16[32,96]{1,0:T(8,128)(2,1)} custom-call(bf16[256,4096]{1,0:T(8,128)(2,1)} %bitcast.2, bf16[256,4096]{1,0:T(8,128)(2,1)} %bitcast.3, bf16[256,128]{1,0:T(8,128)(2,1)} %pin_ref.1, bf16[256,128]{1,0:T(8,128)(2,1)} %pout_ref.1, f32[128,128]{1,0:T(8,128)} %cin_ref.1, f32[128,128]{1,0:T(8,128)} %cout_ref.1, s32[2]{0:T(128)} %len_hbm.1, ...), custom_call_target="tpu_custom_call" | custom-call | tf_op jit(solution)/shard_map/pallas_call | solution.py:335
  38.6 1.3 %copy.11 = bf16[32,96]{1,0:T(8,128)(2,1)} copy(bf16[32,96]{1,0:T(8,128)(2,1)} %shard_map.91) | data formatting | bytes 12288

commit v3 on v2

--- a/solution.py
+++ b/solution.py
@@ -101,21 +101,25 @@
     gathers = []
     own, other = group, 1 - group
 
-    def send(slot_mask, piece, to):
+    half = shard // 2
+
+    def send(slot_mask, piece, part, to):
         slot = xor(me, slot_mask)
+        rows = pl.ds(part * half, half)
         copy = pltpu.make_async_remote_copy(
-            src_ref=g.at[slot, piece], dst_ref=g.at[slot, piece],
-            send_sem=gs_sem.at[len(gathers)], recv_sem=gr_sem.at[slot, piece],
+            src_ref=g.at[slot, piece, rows], dst_ref=g.at[slot, piece, rows],
+            send_sem=gs_sem.at[len(gathers)], recv_sem=gr_sem.at[slot, piece, part],
             device_id=to, device_id_type=MESH,
         )
         copy.start()
         gathers.append(copy)
 
-    def arrived(slot_mask, piece):
+    def arrived(slot_mask, piece, part):
         slot = xor(me, slot_mask)
+        rows = pl.ds(part * half, half)
         pltpu.make_async_remote_copy(
-            src_ref=g.at[slot, piece], dst_ref=g.at[slot, piece],
-            send_sem=gs_sem.at[0], recv_sem=gr_sem.at[slot, piece],
+            src_ref=g.at[slot, piece, rows], dst_ref=g.at[slot, piece, rows],
+            send_sem=gs_sem.at[0], recv_sem=gr_sem.at[slot, piece, part],
             device_id=(group, xor(me, 1)), device_id_type=MESH,
         ).wait_recv()
 
@@ -126,14 +130,14 @@
     fasts = [2 * b for b in range(1, fast)]
     slows = [2 * fast * a for a in range(1, slow)]
     early = slows[:1]
-    for mask in fasts:
-        send(0, own, peer(mask))
-    for mask in slows:
-        send(0, own, peer(mask))
-    for mask in fasts:
-        send(0, other, peer(mask))
-    send(0, own, sibling)
-    send(0, other, sibling)
+    for mask in fasts + slows:
+        for part in range(2):
+            send(0, own, part, peer(mask))
+    for part in range(2):
+        for mask in fasts:
+            send(0, other, part, peer(mask))
+        send(0, own, part, sibling)
+        send(0, other, part, sibling)
 
     for load in loads[5:]:
         load.wait()
@@ -157,41 +161,44 @@
         copy.start()
         id_copies.append(copy)
 
-    def from_slow(mask):
-        arrived(mask, own)
+    def from_slow(mask, part):
+        arrived(mask, own, part)
         for b in fasts:
-            send(mask, own, peer(b))
-        send(mask, own, twin)
-        send(mask, own, sibling)
-
-    def from_fast(mask):
+            send(mask, own, part, peer(b))
+        send(mask, own, part, twin)
+        send(mask, own, part, sibling)
+
+    def from_fast(mask, part):
         for b in fasts:
-            arrived(mask + b, own)
+            arrived(mask + b, own, part)
             if mask and mask not in early:
-                send(mask + b, own, twin)
-            send(mask + b, own, sibling)
-
-    def from_twin(mask):
-        arrived(mask, other)
+                send(mask + b, own, part, twin)
+            send(mask + b, own, part, sibling)
+
+    def from_twin(mask, part):
+        arrived(mask, other, part)
         if mask in early:
             for b in fasts:
-                send(mask, other, peer(b))
-        send(mask, other, sibling)
-
-    def last(mask):
+                send(mask, other, part, peer(b))
+        send(mask, other, part, sibling)
+
+    def last(mask, part):
         for b in fasts:
-            arrived(mask + b, other)
-            send(mask + b, other, sibling)
+            arrived(mask + b, other, part)
+            send(mask + b, other, part, sibling)
 
     span = n // slow * shard
 
-    def project(mask):
+    def project(mask, part):
+        if part == 0:
+            return
         if mask == 0:
             loads[2].wait()
             loads[3].wait()
         for b in [0] + fasts:
             for piece in (own, other):
-                arrived(mask + b + 1, piece)
+                for at in range(2):
+                    arrived(mask + b + 1, piece, at)
         block_at = xor(me // (2 * fast), mask // (2 * fast))
         columns = pl.ds(pl.multiple_of(block_at * span, 128), span)
         shards = pl.ds(block_at * 2 * fast, 2 * fast)
@@ -239,13 +246,17 @@
         k[1] = eliminate_panel(second)
         return carry
 
+    steps = [(event, mask, part) for event, mask in events for part in range(2)]
+    first, busy = panels // 4, max(1, 3 * len(steps) // 4)
     done = 0
-    for at, (event, mask) in enumerate(events):
-        upto = panels * (at + 1) // len(events)
+    for at, (event, mask, part) in enumerate(steps):
+        upto = min(panels, first + (panels - first) * at // busy)
         if upto > done:
             lax.fori_loop(0, upto - done, step, 0)
             done = upto
-        event(mask)
+        event(mask, part)
+    if panels > done:
+        lax.fori_loop(0, panels - done, step, 0)
 
     position = lax.broadcasted_iota(jnp.int32, (length, 1), 0)
     for s in range(seqs):
@@ -353,7 +364,7 @@
                 pltpu.VMEM((n, held, wide), BF16),
                 pltpu.VMEM((n, held, wide), BF16),
                 dma((9,)),
-                dma((2 * n,)), dma((n, 2)), dma((n,)), dma((n,)),
+                dma((4 * n,)), dma((n, 2, 2)), dma((n,)), dma((n,)),
                 dma((n,)), dma((n,)), dma((n,)), dma((n,)),
             ],
             compiler_params=pltpu.CompilerParams(collective_id=0, has_side_effects=True),

time: 40.1 us -> 39.4 us (0.983)
  Pallas kernels: 38.6 us -> 37.9 us
    pallas_call x1, Pallas kernels: 38.6 us -> 37.9 us  [body(): pl.pallas_call(functools.partial(kernel, n, slow, fast), out_shape=jax.Sh...]
where the time goes in v3:
time: 39.4 us; the launch traced here: 39.2 us
  Pallas kernels  37.9 us (96%)
  local copies, waits for them, and re-layouts  1.3 us (3%)
    pallas_call x1, Pallas kernels, body(): pl.pallas_call(functools.partial(kernel, n, slow, fast), out_shape=jax.Sh...  37.9 us
    unnamed x1, local copies, waits for them, and re-layouts  1.3 us

profile of v3, /device:TPU:0, one launch (start us, length us, event | category | flops | bytes accessed | tf_op | source)
XLA Modules:
  0.0 39.2 jit_solution(15828714220738000563)
XLA Ops:
  0.0 37.9 %shard_map.91 = bf16[32,96]{1,0:T(8,128)(2,1)} custom-call(bf16[256,4096]{1,0:T(8,128)(2,1)} %bitcast.2, bf16[256,4096]{1,0:T(8,128)(2,1)} %bitcast.3, bf16[256,128]{1,0:T(8,128)(2,1)} %pin_ref.1, bf16[256,128]{1,0:T(8,128)(2,1)} %pout_ref.1, f32[128,128]{1,0:T(8,128)} %cin_ref.1, f32[128,128]{1,0:T(8,128)} %cout_ref.1, s32[2]{0:T(128)} %len_hbm.1, ...), custom_call_target="tpu_custom_call" | custom-call | tf_op jit(solution)/shard_map/pallas_call | solution.py:346
  37.9 1.3 %copy.11 = bf16[32,96]{1,0:T(8,128)(2,1)} copy(bf16[32,96]{1,0:T(8,128)(2,1)} %shard_map.91) | data formatting | bytes 12288
